TPU v7x, 256 devices: a whole 4x4x8 slice. The times are simulated.
256 devices in a mesh: dp: 4 (over y), space: 64 (over x, z, core).
Axes of the slice: x: 4, y: 4, z: 8, core: 2. Of those that a mesh axis runs over, the one named last changes fastest.
Arguments:
- volume: bfloat16 [4, 128, 4, 64, 128], P('dp', 'space'), may hold values from -30 to 30
- weights_one: bfloat16 [3, 3, 3, 128, 256], replicated, may hold values from -0.109375 to 0.109375
- gain_one: float32 [256], replicated, may hold values from 0.1 to 1.9
- shift_one: float32 [256], replicated, may hold values from -3 to 3
- weights_two: bfloat16 [3, 3, 3, 8, 256], P(None, None, None, None, 'space'), may hold values from -0.4375 to 0.4375
- gain_two: float32 [256], P('space'), may hold values from 0.1 to 1.9
- shift_two: float32 [256], P('space'), may hold values from -3 to 3
- upstream: bfloat16 [4, 256, 64, 2, 32], P('dp', 'space'), may hold values from -6 to 6
Outputs:
- result: bfloat16 [4, 256, 64, 2, 32], P('dp', 'space')
- grad_weights_one: float32 [3, 3, 3, 128, 256], P(None, None, None, None, 'space')
- grad_weights_two: float32 [3, 3, 3, 8, 256], P(None, None, None, None, 'space')
All inputs are finite; a program needn't handle non-finite values.
Results may differ from a plain program's by a relative error of at most 0.0057.
Values may be sent and summed in bfloat16 or wider, within the bound.
A program may use at most 64 MiB of HBM per device.

v0:
```python
import math
import jax
import jax.numpy as jnp
from jax import lax
from jax.sharding import PartitionSpec as P

EPS = 1e-05
LAST = ("NDHWC", "DHWIO", "NDHWC")
FIRST = ("NCDHW", "DHWIO", "NCDHW")


def from_behind(value, axis, steps):
    count = lax.axis_size(axis)
    leading, last = (max(0, -steps), min(count, count - steps))
    return lax.ppermute(value, axis, [(source, source + steps) for source in range(leading, last)])


def combined_all(part, axis, combine):
    gathered = jax.tree.map(lambda a: lax.all_gather(a, axis), part)

    def take(source):
        return jax.tree.map(lambda a: lax.dynamic_index_in_dim(a, source, 0, False), gathered)

    return lax.fori_loop(
        1, lax.axis_size(axis), lambda source, state: combine(state, take(source)), take(0)
    )


def welford(left, right):
    count_a, mean_a, spread_a = left
    count_b, mean_b, spread_b = right
    merged = count_a + count_b
    delta = mean_b - mean_a
    return (
        merged,
        mean_a + delta * (count_b / merged),
        spread_a + spread_b + delta * delta * (count_a * count_b / merged),
    )


def group_filter(inputs, grads):
    return lax.conv_general_dilated(
        inputs,
        grads,
        (1, 1, 1),
        ((1, 1), (1, 1), (1, 1)),
        dimension_numbers=("CNDHW", "IODHW", "DHWNC"),
        preferred_element_type=jnp.float32,
    )


def per_device(
    volume, weights_one, gain_one, shift_one, weights_two, gain_two, shift_two, upstream
):
    planes = lax.axis_size("space")
    below = from_behind(volume[:, 1:], "space", 1)
    stacked = jnp.concatenate([below, volume], axis=1)
    pre_one = lax.conv_general_dilated(
        stacked,
        weights_one,
        (2, 2, 2),
        ((0, 0), (1, 1), (1, 1)),
        dimension_numbers=LAST,
        preferred_element_type=jnp.float32,
    )
    lead = pre_one.shape[0]
    count = float(lax.axis_size("dp") * lead * planes * pre_one.shape[2] * pre_one.shape[3])
    axes_last = (0, 1, 2, 3)
    mean_one = lax.psum(jnp.sum(pre_one, axis=axes_last), ("dp", "space")) / count
    spread_one = lax.psum(jnp.sum(jnp.square(pre_one - mean_one), axis=axes_last), ("dp", "space"))
    var_one = spread_one / count
    inv_one = lax.rsqrt(var_one + EPS)
    norm_one = (pre_one - mean_one) * inv_one
    act_in = norm_one * gain_one + shift_one
    activated = jax.nn.silu(act_in).astype(jnp.bfloat16)
    act_first = jnp.transpose(activated, (0, 4, 1, 2, 3))
    own_width = weights_two.shape[4]
    group_width = weights_two.shape[3]
    window = max(own_width, group_width)
    replicas = window // own_width
    channels = act_first.shape[1]
    tail = act_first.shape[2:]
    parts = act_first.reshape((lead, channels // window, 1, window) + tail)
    copies = jnp.broadcast_to(parts, (lead, channels // window, replicas, window) + tail)
    outgoing = copies.reshape((lead, planes * window) + tail)
    inputs = lax.all_to_all(outgoing, "space", split_axis=1, concat_axis=2, tiled=True)
    groups_here = window // group_width
    per_group = own_width // groups_here
    padding_one = ((1, 1), (1, 1), (1, 1))
    pre_two = lax.conv_general_dilated(
        inputs,
        weights_two,
        (1, 1, 1),
        padding_one,
        dimension_numbers=FIRST,
        feature_group_count=groups_here,
        preferred_element_type=jnp.float32,
    )
    axes_first = (0, 2, 3, 4)
    local_mean_two = jnp.mean(pre_two, axis=axes_first, keepdims=True)
    local_spread_two = jnp.sum(jnp.square(pre_two - local_mean_two), axis=axes_first, keepdims=True)
    local_count_two = float(pre_two.size // pre_two.shape[1])
    merged_two, mean_two, spread_two = combined_all(
        (jnp.full((1, 1, 1, 1, 1), local_count_two, jnp.float32), local_mean_two, local_spread_two),
        "dp",
        welford,
    )
    inv_two = lax.rsqrt(spread_two / merged_two + EPS)
    norm_two = (pre_two - mean_two) * inv_two
    gain_col = gain_two.reshape((1, -1, 1, 1, 1))
    shift_col = shift_two.reshape((1, -1, 1, 1, 1))
    result = (norm_two * gain_col + shift_col).astype(jnp.bfloat16)
    grad_norm_two = upstream.astype(jnp.float32) * gain_col * (1.0 / math.sqrt(count))
    first_sum, second_sum = lax.psum(
        (
            jnp.sum(grad_norm_two, axis=axes_first, keepdims=True),
            jnp.sum(grad_norm_two * norm_two, axis=axes_first, keepdims=True),
        ),
        "dp",
    )
    grad_pre_two = (
        inv_two * (grad_norm_two - first_sum / count - norm_two * (second_sum / count))
    ).astype(jnp.bfloat16)
    grouped_inputs = inputs.reshape((lead, groups_here, group_width) + inputs.shape[2:])
    grouped_grads = grad_pre_two.reshape((lead, groups_here, per_group) + grad_pre_two.shape[2:])
    pieces = jax.vmap(group_filter, in_axes=(1, 1))(grouped_inputs, grouped_grads)
    local_two = jnp.transpose(pieces, (1, 2, 3, 4, 0, 5)).reshape((3, 3, 3, group_width, own_width))
    grad_weights_two = lax.psum(local_two, "dp")
    flipped = weights_two[::-1, ::-1, ::-1]
    turned = (
        flipped.reshape((3, 3, 3, group_width, groups_here, per_group))
        .transpose((0, 1, 2, 5, 4, 3))
        .reshape((3, 3, 3, per_group, window))
    )
    partial_grad = lax.conv_general_dilated(
        grad_pre_two,
        turned,
        (1, 1, 1),
        padding_one,
        dimension_numbers=FIRST,
        feature_group_count=groups_here,
        preferred_element_type=jnp.float32,
    )
    arrived = lax.all_to_all(partial_grad, "space", split_axis=2, concat_axis=1, tiled=True)
    grad_act = jnp.sum(
        arrived.reshape((lead, channels // window, replicas, window) + arrived.shape[2:]), axis=2
    ).reshape((lead, channels) + arrived.shape[2:])
    grad_last = jnp.transpose(grad_act, (0, 2, 3, 4, 1))
    sigma = jax.nn.sigmoid(act_in)
    grad_norm_one = grad_last * (sigma * (1.0 + act_in * (1.0 - sigma))) * gain_one
    third_sum, fourth_sum = lax.psum(
        (jnp.sum(grad_norm_one, axis=axes_last), jnp.sum(grad_norm_one * norm_one, axis=axes_last)),
        ("dp", "space"),
    )
    grad_pre_one = (
        inv_one * (grad_norm_one - third_sum / count - norm_one * (fourth_sum / count))
    ).astype(jnp.bfloat16)
    local_one = lax.conv_general_dilated(
        stacked,
        grad_pre_one,
        (1, 1, 1),
        ((0, 0), (1, 0), (1, 0)),
        rhs_dilation=(2, 2, 2),
        dimension_numbers=("CDHWN", "IDHWO", "DHWNC"),
        preferred_element_type=jnp.float32,
    )
    summed = lax.psum(local_one, "dp")
    grad_weights_one = lax.psum_scatter(summed, "space", scatter_dimension=4, tiled=True)
    return (result, grad_weights_one, grad_weights_two)


def solution(mesh):
    return jax.shard_map(
        per_device,
        mesh=mesh,
        in_specs=(
            P("dp", "space", None, None, None),
            P(),
            P(),
            P(),
            P(None, None, None, None, "space"),
            P("space"),
            P("space"),
            P("dp", "space", None, None, None),
        ),
        out_specs=(
            P("dp", "space", None, None, None),
            P(None, None, None, None, "space"),
            P(None, None, None, None, "space"),
        ),
        check_vma=False,
    )
```

profile of v0, /device:TPU:2, one launch (start us, length us, event | category | flops | bytes accessed | tf_op | source)
XLA Modules:
  0.0 559.2 jit_solution(1003987523249396105)
XLA Ops:
  8.3 1.9 collective-permute-start
  10.2 7.9 %collective-permute-done = bf16[1,1,4,64,128]{4,0,3,2,1:T(2,128)(2,1)S(1)} collective-permute-done((bf16[1,1,4,64,128]{4,0,3,2,1:T(2,128)(2,1)S(1)}, bf16[1,1,4,64,128]{4,0,3,2,1:T(2,128)(2,1)S(1)}, u32[]{:S(2)}, u32[]{:S(2)}) %collective-permute-start) | collective-permute-done | bytes 65568 | tf_op jit(solution)/shard_map/ppermute | solution.py:15
  21.0 74.9 %psum.56 = f32[256]{0:T(256)S(1)} all-reduce(f32[256]{0:T(256)S(1)} %get-tuple-element.289), channel_id=1, replica_groups=mesh['dp'=4,'space'=64] {'dp','space'}, use_global_device_ids=true, to_apply=%region_1.0 | all-reduce | flops 256 | bytes 2048 | tf_op jit(solution)/shard_map/psum | solution.py:69
  95.9 74.4 %psum.57 = f32[256]{0:T(256)S(1)} all-reduce(f32[256]{0:T(256)S(1)} %select_reduce_fusion.2), channel_id=1, replica_groups=mesh['dp'=4,'space'=64] {'dp','space'}, use_global_device_ids=true, to_apply=%region_3.0 | all-reduce | flops 256 | bytes 2048 | tf_op jit(solution)/shard_map/psum | solution.py:70
  172.2 8.1 %all-to-all-start = ((bf16[64,2,256]{2,1,0:T(2,128)(2,1)}), bf16[64,2,256]{2,1,0:T(2,128)(2,1)S(1)}, u32[]{:S(2)}, u32[]{:S(2)}) async-start(bf16[64,2,256]{2,1,0:T(2,128)(2,1)} %reshape.180), calls=%async_computation | async-start | bytes 131072 | tf_op jit(solution)/shard_map/all_to_all | solution.py:86
  183.0 6.0 %all-to-all-done = bf16[64,2,256]{2,1,0:T(2,128)(2,1)S(1)} async-done(((bf16[64,2,256]{2,1,0:T(2,128)(2,1)}), bf16[64,2,256]{2,1,0:T(2,128)(2,1)S(1)}, u32[]{:S(2)}, u32[]{:S(2)}) %all-to-all-start) | async-done | bytes 65568 | tf_op jit(solution)/shard_map/all_to_all | solution.py:86
  190.2 2.1 copy.207
  192.5 5.6 fusion.8
  198.1 1.7 copy.208
  200.5 8.6 %all-reduce.7 = (f32[4]{0:T(128)S(1)}, f32[16]{0:T(128)S(1)}, f32[16]{0:T(128)S(1)}) all-reduce(f32[4]{0:T(128)S(1)} %dynamic-update-slice, f32[16]{0:T(128)S(1)} %get-tuple-element.288, f32[16]{0:T(128)S(1)} %dynamic-update-slice.2), channel_id=1, replica_groups=mesh['dp'=4,'space'=64] {'dp'}, use_global_device_ids=true, to_apply=%add | all-reduce | flops 36 | bytes 288
  209.8 13.6 %while.19 = (s32[]{:T(128)}, f32[1,1,1,1,1]{4,3,2,1,0:T(1,128)}, f32[1,4,1,1,1]{1,4,3,2,0:T(1,128)S(1)}, f32[1,4,1,1,1]{1,4,3,2,0:T(1,128)S(1)}, f32[4,1,1,1,1,1...) while((s32[]{:T(128)}, f32[1,1,1,1,1]{4,3,2,1,0:T(1,128)}, ...), condition=%wide.region_7.8_spmd, body=%wide.region_6.7_spmd.sunk | while | flops 37 | bytes 303 | solution.py:24
  225.2 9.4 %all-reduce.6 = (f32[1,4,1,1,1]{1,4,3,2,0:T(1,128)S(1)}, f32[1,4,1,1,1]{1,4,3,2,0:T(1,128)S(1)}) all-reduce(f32[1,4,1,1,1]{1,4,3,2,0:T(1,128)S(1)} %bitcast.177, f32[1,4,1,1,1]{1,4,3,2,0:T(1,128)S(1)} %bitcast.176), channel_id=1, replica_groups=mesh['dp'=4,'space'=64] {'dp'}, use_global_device_ids=true, to_apply=%region_11.12 | all-reduce | flops 8 | bytes 64 | tf_op jit(solution)/shard_map/psum | solution.py:114
  235.5 6.9 %convolution_select_fusion = f32[64,2,8,5,8]{4,2,3,1,0:T(8,128)} fusion(pred[8,5]{0,1:T(8,128)(4,1)S(1)} %copy-done.7, bf16[4,64,2,1,7,2]{4,0,5,2,1,3:T(4,128)(2,1)S(1)} %slice.28, bf16[4,64,2,1,8,5]{4,0,5,2,1,3:T(4,128)(2,1)S(1)} %copy.218, bf16[3,3,3,8,4]{3,4,2,1,0:T(4,128)(2,1)S(1)} %copy-done.6), kind=kOutput, calls=%fused_computation.19 | convolution fusion | flops 6049792 | bytes 220904 | tf_op jit(solution)/shard_map/conv_general_dilated | solution.py:135
  242.5 2.6 copy.219
  246.4 5.5 all-to-all-start.1
  253.0 8.2 %all-to-all-done.1 = f32[64,1,512]{2,1,0:T(1,128)S(1)} async-done(((f32[64,1,512]{2,1,0:T(1,128)}), f32[64,1,512]{2,1,0:T(1,128)S(1)}, u32[]{:S(2)}, u32[]{:S(2)}) %all-to-all-start.1) | async-done | bytes 131104 | tf_op jit(solution)/shard_map/all_to_all | solution.py:144
  263.6 1.3 fusion.51
  264.9 73.3 %all-reduce.4 = (f32[256]{0:T(256)S(1)}, f32[256]{0:T(256)S(1)}) all-reduce(f32[256]{0:T(256)S(1)} %get-tuple-element.252, f32[256]{0:T(256)S(1)} %get-tuple-element.251), channel_id=1, replica_groups=mesh['dp'=4,'space'=64] {'dp','space'}, use_global_device_ids=true, to_apply=%region_16.17 | all-reduce | flops 512 | bytes 4096 | tf_op jit(solution)/shard_map/psum | solution.py:151
  339.4 2.8 fusion.53
  344.1 3.5 copy.231
  348.3 3.4 copy.230
  351.7 29.6 %fusion.54 = f32[3,3,3,8,4]{3,4,2,1,0:T(4,128)S(1)} fusion(bf16[1,8,64,2,32]{1,0,4,3,2:T(2,128)(2,1)} %copy.230, bf16[1,4,64,2,32]{1,0,4,3,2:T(2,128)(2,1)} %copy.231), kind=kOutput, calls=%fused_computation.97 | convolution fusion | flops 4572160 | bytes 101760 | tf_op jit(solution)/shard_map/vmap()/conv_general_dilated | solution.py:42
  381.3 151.0 %all-reduce.10.cloned.1.call-done = f32[3,3,3,128,256]{3,4,2,1,0:T(8,128)} async-done(((f32[3,3,3,128,256]{3,4,2,1,0:T(8,128)}), f32[3,3,3,128,256]{3,4,2,1,0:T(8,128)}) %all-reduce.10.cloned.1.call-update) | async-done | bytes 3538960
  533.3 18.7 %all-reduce.5 = (f32[3,3,3,128,4]{3,4,2,1,0:T(4,128)}, f32[3,3,3,8,4]{3,4,2,1,0:T(4,128)}) all-reduce(f32[3,3,3,128,4]{3,4,2,1,0:T(4,128)S(1)} %constant_dynamic-slice_fusion.3, f32[3,3,3,8,4]{3,4,2,1,0:T(4,128)S(1)} %fusion.54), channel_id=1, replica_groups=mesh['dp'=4,'space'=64] {'dp'}, use_global_device_ids=true, to_apply=%region_17.18 | all-reduce | flops 14688 | bytes 117504 | tf_op jit(solution)/shard_map/psum | solution.py:167
  (115 shorter events, 23.4 us)
Async XLA Ops:
  7.2 13.3 %copy-start = (bf16[3,3,3,128,256]{4,3,2,1,0:T(8,128)(2,1)S(1)}, bf16[3,3,3,128,256]{4,3,2,1,0:T(8,128)(2,1)}, u32[]{:S(2)}) copy-start(bf16[3,3,3,128,256]{4,3,2,1,0:T(8,128)(2,1)} %param.11) | copy-start | bytes 5308420
  7.2 13.3 %copy-start.7 = (pred[8,5]{0,1:T(8,128)(4,1)S(1)}, pred[8,5]{0,1:T(8,128)(4,1)}, u32[]{:S(2)}) copy-start(pred[8,5]{0,1:T(8,128)(4,1)} %constant.99) | copy-start | bytes 124
  8.3 9.8 %collective-permute-start = (bf16[1,1,4,64,128]{4,0,3,2,1:T(2,128)(2,1)S(1)}, bf16[1,1,4,64,128]{4,0,3,2,1:T(2,128)(2,1)S(1)}, u32[]{:S(2)}, u32[]{:S(2)}) collective-permute-start(bf16[1,1,4,64,128]{4,0,3,2,1:T(2,128)(2,1)S(1)} %copy.254), channel_id=1, source_target_pairs={{0,1},{1,2},{2,3},{3,4},{4,5},{5,6},{6,7},{7,8},{8,9},{9,10},{10,1... | collective-permute-start | bytes 196616 | tf_op jit(solution)/shard_map/ppermute | solution.py:15
  19.4 0.7 copy-start.1
  20.1 150.2 %copy-start.8 = (f32[256]{0:T(256)S(1)}, f32[256]{0:T(256)}, u32[]{:S(2)}) copy-start(f32[256]{0:T(256)} %param.12) | copy-start | bytes 3076
  20.1 150.2 %copy-start.11 = (f32[256]{0:T(256)S(1)}, f32[256]{0:T(256)}, u32[]{:S(2)}) copy-start(f32[256]{0:T(256)} %param.13) | copy-start | bytes 3076
  20.5 159.8 %copy-start.5 = (bf16[3,3,3,8,4]{3,4,2,1,0:T(4,128)(2,1)S(1)}, bf16[3,3,3,8,4]{3,4,2,1,0:T(4,128)(2,1)}, u32[]{:S(2)}) copy-start(bf16[3,3,3,8,4]{3,4,2,1,0:T(4,128)(2,1)} %param.14) | copy-start | bytes 5188
  20.5 160.4 %copy-start.14 = (u32[256]{0:T(256)S(1)}, u32[256]{0:T(256)}, u32[]{:S(2)}) copy-start(u32[256]{0:T(256)} %constant.108) | copy-start | bytes 3076
  170.3 0.6 copy-start.9
  172.2 16.9 %all-to-all-start = ((bf16[64,2,256]{2,1,0:T(2,128)(2,1)}), bf16[64,2,256]{2,1,0:T(2,128)(2,1)S(1)}, u32[]{:S(2)}, u32[]{:S(2)}) async-start(bf16[64,2,256]{2,1,0:T(2,128)(2,1)} %reshape.180), calls=%async_computation | async-start | bytes 131072 | tf_op jit(solution)/shard_map/all_to_all | solution.py:86
  198.1 26.0 %copy-start.10 = (f32[4]{0:T(128)S(1)}, f32[4]{0:T(128)}, u32[]{:S(2)}) copy-start(f32[4]{0:T(128)} %param.15) | copy-start | bytes 52
  198.1 26.1 %copy-start.12 = (f32[4]{0:T(128)S(1)}, f32[4]{0:T(128)}, u32[]{:S(2)}) copy-start(f32[4]{0:T(128)} %param.16) | copy-start | bytes 52
  198.1 26.9 %copy-start.4 = (bf16[1,4,64,2,32]{2,4,3,1,0:T(8,128)(2,1)S(1)}, bf16[1,4,64,2,32]{2,4,3,1,0:T(8,128)(2,1)}, u32[]{:S(2)}) copy-start(bf16[1,4,64,2,32]{2,4,3,1,0:T(8,128)(2,1)} %param.17) | copy-start | bytes 98308
  199.8 35.7 %copy-start.6 = (bf16[3,3,3,8,4]{3,4,2,1,0:T(4,128)(2,1)S(1)}, bf16[3,3,3,8,4]{3,4,2,1,0:T(4,128)(2,1)}, u32[]{:S(2)}) copy-start(bf16[3,3,3,8,4]{3,4,2,1,0:T(4,128)(2,1)} %rev.3) | copy-start | bytes 5188
  246.4 14.9 %all-to-all-start.1 = ((f32[64,1,512]{2,1,0:T(1,128)}), f32[64,1,512]{2,1,0:T(1,128)S(1)}, u32[]{:S(2)}, u32[]{:S(2)}) async-start(f32[64,1,512]{2,1,0:T(1,128)} %reshape.182), calls=%async_computation.1 | async-start | bytes 262144 | tf_op jit(solution)/shard_map/all_to_all | solution.py:144
  251.8 280.5 %all-reduce.10.cloned.1.call-start = ((), (), s32[]{:S(2)}) async-start(), calls=%async_computation.2 | async-start | bytes 7077888
  262.7 76.7 %copy-start.2 = (bf16[1,3,4,64,128]{4,0,3,2,1:T(2,128)(2,1)S(1)}, bf16[1,3,4,64,128]{4,0,3,2,1:T(2,128)(2,1)}, u32[]{:S(2)}) copy-start(bf16[1,3,4,64,128]{4,0,3,2,1:T(2,128)(2,1)} %copy-done.1) | copy-start | bytes 589828
  342.2 0.7 copy-start.13
  342.2 5.4 copy-start.3
Sparse Core Ops, SparseCore 0:
  342.4 189.9 all-reduce.9
where the time goes:
time: 568 us; the launch traced here: 559 us
  blocking collectives  259 us (46%)
  waiting for transfers between devices  173 us (30%)
  matrix products  45.4 us (8%)
  local copies, waits for them, and re-layouts  31 us (5%)
  between operations  16.8 us (3%)
  starting transfers between devices  15.5 us (3%)
  loops' own time  11.6 us (2%)
  other arithmetic  6.47 us (1%)
    unnamed x2, waiting for transfers between devices  151 us
    psum x1, blocking collectives, per_device(): lax.psum(jnp.sum(pre_one, axis=axes_last), ('dp', 'space')) / count  74.9 us
    psum x1, blocking collectives, per_device(): lax.psum(jnp.sum(jnp.square(pre_one - mean_one), axis=axes_last), ('dp',...  74.4 us
    psum x1, blocking collectives, per_device(): lax.psum((jnp.sum(grad_norm_one, axis=axes_last), jnp.sum(grad_norm_one *...  73.3 us
    conv_general_dilated x1, matrix products, group_filter(): lax.conv_general_dilated(inputs, grads, (1, 1, 1), ((1, 1), (1, 1), (1, 1...  29.6 us
    psum x1, blocking collectives, per_device(): summed = lax.psum(local_one, 'dp')  18.7 us
    another operation x1, loops' own time, combined_all(): lax.fori_loop(1, lax.axis_size(axis), lambda source, state: combine(state...  11.6 us
  transfers between devices with their start and end apart: 4, of which 4 were waited for; matrix products, arithmetic and copies ran while one was open for 7% of the time, Pallas kernels for 0%

commit v1 on v0

--- a/solution.py
+++ b/solution.py
@@ -1,3 +1,4 @@
+import functools
 import math
 import jax
 import jax.numpy as jnp
@@ -7,6 +8,20 @@
 EPS = 1e-05
 LAST = ("NDHWC", "DHWIO", "NDHWC")
 FIRST = ("NCDHW", "DHWIO", "NCDHW")
+
+
+def _plan_routes_all(v0, dev_axis):
+    how_many = jax.lax.axis_size(dev_axis)
+    big = lambda response: [(m, m ^ response) for m in range(how_many)]
+    raw_out = v0
+    for it in range(how_many.bit_length() - 1):
+        t1 = big(1 << it)
+        z2 = jax.lax.ppermute(raw_out, dev_axis, t1)
+        raw_out = raw_out + z2
+    return raw_out
+
+
+draft_bands = functools.partial(_plan_routes_all, dev_axis="dp")
 
 
 def from_behind(value, axis, steps):
@@ -164,7 +179,7 @@
         dimension_numbers=("CDHWN", "IDHWO", "DHWNC"),
         preferred_element_type=jnp.float32,
     )
-    summed = lax.psum(local_one, "dp")
+    summed = draft_bands(local_one)
     grad_weights_one = lax.psum_scatter(summed, "space", scatter_dimension=4, tiled=True)
     return (result, grad_weights_one, grad_weights_two)
 

time: 568 us -> 727 us (1.28)
  waiting for transfers between devices: 173 us -> 317 us
  starting transfers between devices: 15.5 us -> 26.8 us
    ppermute x0 -> x2, waiting for transfers between devices: none -> 156 us  [_plan_routes_all(): z2 = jax.lax.ppermute(raw_out, dev_axis, t1)]
    unnamed x2, waiting for transfers between devices: 151 us -> 137 us
    ppermute x0 -> x2, starting transfers between devices: none -> 11.3 us  [_plan_routes_all(): z2 = jax.lax.ppermute(raw_out, dev_axis, t1)]
  transfers between devices with their start and end apart: 4 -> 6, of which waited for: 4 -> 6; matrix products, arithmetic and copies ran while one was open for 7% -> 5% of each run, Pallas kernels for 0% -> 0%
where the time goes in v1:
time: 727 us; the launch traced here: 718 us
  waiting for transfers between devices  317 us (44%)
  blocking collectives  257 us (35%)
  matrix products  44.6 us (6%)
  local copies, waits for them, and re-layouts  35.7 us (5%)
  starting transfers between devices  26.8 us (4%)
  between operations  16.8 us (2%)
  loops' own time  11.4 us (2%)
  other arithmetic  9.12 us (1%)
    ppermute x2, waiting for transfers between devices, _plan_routes_all(): z2 = jax.lax.ppermute(raw_out, dev_axis, t1)  156 us
    unnamed x2, waiting for transfers between devices  137 us
    psum x1, blocking collectives, per_device(): lax.psum(jnp.sum(pre_one, axis=axes_last), ('dp', 'space')) / count  74.9 us
    psum x1, blocking collectives, per_device(): lax.psum(jnp.sum(jnp.square(pre_one - mean_one), axis=axes_last), ('dp',...  74.4 us
    psum x1, blocking collectives, per_device(): lax.psum((jnp.sum(grad_norm_one, axis=axes_last), jnp.sum(grad_norm_one *...  73.3 us
    conv_general_dilated x1, matrix products, group_filter(): lax.conv_general_dilated(inputs, grads, (1, 1, 1), ((1, 1), (1, 1), (1, 1...  29.6 us
    psum x1, blocking collectives, per_device(): grad_weights_two = lax.psum(local_two, 'dp')  16.6 us
  transfers between devices with their start and end apart: 6, of which 6 were waited for; matrix products, arithmetic and copies ran while one was open for 5% of the time, Pallas kernels for 0%

profile of v1, /device:TPU:2, one launch (start us, length us, event | category | flops | bytes accessed | tf_op | source)
XLA Modules:
  0.0 718.2 jit_solution(3796037877745886450)
XLA Ops:
  10.2 7.9 %collective-permute-done = bf16[1,1,4,64,128]{4,0,3,2,1:T(2,128)(2,1)S(1)} collective-permute-done((bf16[1,1,4,64,128]{4,0,3,2,1:T(2,128)(2,1)S(1)}, bf16[1,1,4,64,128]{4,0,3,2,1:T(2,128)(2,1)S(1)}, u32[]{:S(2)}, u32[]{:S(2)}) %collective-permute-start) | collective-permute-done | bytes 65568 | tf_op jit(solution)/shard_map/ppermute | solution.py:30
  20.9 74.9 %psum.49 = f32[256]{0:T(256)S(1)} all-reduce(f32[256]{0:T(256)S(1)} %get-tuple-element.290), channel_id=1, replica_groups=mesh['dp'=4,'space'=64] {'dp','space'}, use_global_device_ids=true, to_apply=%region_1.0 | all-reduce | flops 256 | bytes 2048 | tf_op jit(solution)/shard_map/psum | solution.py:84
  95.9 74.4 %psum.50 = f32[256]{0:T(256)S(1)} all-reduce(f32[256]{0:T(256)S(1)} %select_reduce_fusion.2), channel_id=1, replica_groups=mesh['dp'=4,'space'=64] {'dp','space'}, use_global_device_ids=true, to_apply=%region_3.0 | all-reduce | flops 256 | bytes 2048 | tf_op jit(solution)/shard_map/psum | solution.py:85
  172.4 8.1 %all-to-all-start = ((bf16[64,2,256]{2,1,0:T(2,128)(2,1)}), bf16[64,2,256]{2,1,0:T(2,128)(2,1)S(1)}, u32[]{:S(2)}, u32[]{:S(2)}) async-start(bf16[64,2,256]{2,1,0:T(2,128)(2,1)} %reshape.178), calls=%async_computation | async-start | bytes 131072 | tf_op jit(solution)/shard_map/all_to_all | solution.py:101
  182.5 6.8 all-to-all-done
  192.7 5.6 fusion.8
  200.7 8.6 %all-reduce.6 = (f32[4]{0:T(128)S(1)}, f32[16]{0:T(128)S(1)}, f32[16]{0:T(128)S(1)}) all-reduce(f32[4]{0:T(128)S(1)} %dynamic-update-slice, f32[16]{0:T(128)S(1)} %get-tuple-element.289, f32[16]{0:T(128)S(1)} %dynamic-update-slice.2), channel_id=1, replica_groups=mesh['dp'=4,'space'=64] {'dp'}, use_global_device_ids=true, to_apply=%add | all-reduce | flops 36 | bytes 288
  210.0 13.2 %while.19 = (s32[]{:T(128)}, f32[1,1,1,1,1]{4,3,2,1,0:T(1,128)}, f32[1,4,1,1,1]{1,4,3,2,0:T(1,128)S(1)}, f32[1,4,1,1,1]{1,4,3,2,0:T(1,128)S(1)}, f32[4,1,1,1,1,1...) while((s32[]{:T(128)}, f32[1,1,1,1,1]{4,3,2,1,0:T(1,128)}, ...), condition=%wide.region_7.8_spmd, body=%wide.region_6.7_spmd.sunk | while | flops 37 | bytes 303 | solution.py:39
  225.0 9.2 %all-reduce.5 = (f32[1,4,1,1,1]{1,4,3,2,0:T(1,128)S(1)}, f32[1,4,1,1,1]{1,4,3,2,0:T(1,128)S(1)}) all-reduce(f32[1,4,1,1,1]{1,4,3,2,0:T(1,128)S(1)} %bitcast.175, f32[1,4,1,1,1]{1,4,3,2,0:T(1,128)S(1)} %bitcast.174), channel_id=1, replica_groups=mesh['dp'=4,'space'=64] {'dp'}, use_global_device_ids=true, to_apply=%region_11.12 | all-reduce | flops 8 | bytes 64 | tf_op jit(solution)/shard_map/psum | solution.py:129
  235.1 6.9 convolution_select_fusion
  242.0 2.7 copy.228
  245.9 5.5 all-to-all-start.1
  251.9 8.9 %all-to-all-done.1 = f32[64,1,512]{2,1,0:T(1,128)S(1)} async-done(((f32[64,1,512]{2,1,0:T(1,128)}), f32[64,1,512]{2,1,0:T(1,128)S(1)}, u32[]{:S(2)}, u32[]{:S(2)}) %all-to-all-start.1) | async-done | bytes 131104 | tf_op jit(solution)/shard_map/all_to_all | solution.py:159
  264.3 73.3 %all-reduce.4 = (f32[256]{0:T(256)S(1)}, f32[256]{0:T(256)S(1)}) all-reduce(f32[256]{0:T(256)S(1)} %get-tuple-element.255, f32[256]{0:T(256)S(1)} %get-tuple-element.254), channel_id=1, replica_groups=mesh['dp'=4,'space'=64] {'dp','space'}, use_global_device_ids=true, to_apply=%region_16.17 | all-reduce | flops 512 | bytes 4096 | tf_op jit(solution)/shard_map/psum | solution.py:166
  340.3 78.2 %collective-permute-done.1 = f32[3,3,3,128,256]{4,3,2,1,0:T(8,128)S(1)} collective-permute-done((f32[3,3,3,128,256]{4,3,2,1,0:T(8,128)S(1)}, f32[3,3,3,128,256]{4,3,2,1,0:T(8,128)S(1)}, u32[]{:S(2)}, u32[]{:S(2)}) %collective-permute-start.1) | collective-permute-done | bytes 3538976 | tf_op jit(solution)/shard_map/ppermute | solution.py:19
  419.2 11.2 %collective-permute-start.2 = (f32[3,3,3,128,256]{4,3,2,1,0:T(8,128)S(1)}, f32[3,3,3,128,256]{4,3,2,1,0:T(8,128)S(1)}, u32[]{:S(2)}, u32[]{:S(2)}) collective-permute-start(f32[3,3,3,128,256]{4,3,2,1,0:T(8,128)S(1)} %add.153), channel_id=1, source_target_pairs={{0,128},{64,192},{128,0},{192,64},{1,129},{65,193},{129,1},{193,65... | collective-permute-start | bytes 10616840 | tf_op jit(solution)/shard_map/ppermute | solution.py:19
  430.4 77.5 %collective-permute-done.2 = f32[3,3,3,128,256]{4,3,2,1,0:T(8,128)S(1)} collective-permute-done((f32[3,3,3,128,256]{4,3,2,1,0:T(8,128)S(1)}, f32[3,3,3,128,256]{4,3,2,1,0:T(8,128)S(1)}, u32[]{:S(2)}, u32[]{:S(2)}) %collective-permute-start.2) | collective-permute-done | bytes 3538976 | tf_op jit(solution)/shard_map/ppermute | solution.py:19
  507.8 2.2 add.154
  510.1 6.4 copy.238
  518.4 3.4 copy.241
  522.5 3.2 copy.240
  525.7 29.6 %fusion.54 = f32[3,3,3,8,4]{3,4,2,1,0:T(4,128)S(1)} fusion(bf16[1,8,64,2,32]{1,0,4,3,2:T(2,128)(2,1)} %copy.240, bf16[1,4,64,2,32]{1,0,4,3,2:T(2,128)(2,1)} %copy.241), kind=kOutput, calls=%fused_computation.97 | convolution fusion | flops 4572160 | bytes 101760 | tf_op jit(solution)/shard_map/vmap()/conv_general_dilated | solution.py:57
  555.3 16.6 %psum.55 = f32[3,3,3,8,4]{3,4,2,1,0:T(4,128)} all-reduce(f32[3,3,3,8,4]{3,4,2,1,0:T(4,128)S(1)} %fusion.54), channel_id=1, replica_groups=mesh['dp'=4,'space'=64] {'dp'}, use_global_device_ids=true, to_apply=%region_18.19 | all-reduce | flops 864 | bytes 6912 | tf_op jit(solution)/shard_map/psum | solution.py:143
  572.0 137.4 %all-reduce.9.cloned.1.call-done = f32[3,3,3,128,256]{3,2,1,0,4:T(4,128)} async-done(((f32[3,3,3,128,256]{3,2,1,0,4:T(4,128)}), f32[3,3,3,128,256]{3,2,1,0,4:T(4,128)}) %all-reduce.9.cloned.1.call-update) | async-done | bytes 3538960
  (119 shorter events, 31.5 us)
Async XLA Ops:
  7.2 13.3 %copy-start = (bf16[3,3,3,128,256]{4,3,2,1,0:T(8,128)(2,1)S(1)}, bf16[3,3,3,128,256]{4,3,2,1,0:T(8,128)(2,1)}, u32[]{:S(2)}) copy-start(bf16[3,3,3,128,256]{4,3,2,1,0:T(8,128)(2,1)} %param.11) | copy-start | bytes 5308420
  7.2 13.3 %copy-start.6 = (pred[8,5]{0,1:T(8,128)(4,1)S(1)}, pred[8,5]{0,1:T(8,128)(4,1)}, u32[]{:S(2)}) copy-start(pred[8,5]{0,1:T(8,128)(4,1)} %constant.99) | copy-start | bytes 124
  8.3 9.8 %collective-permute-start = (bf16[1,1,4,64,128]{4,0,3,2,1:T(2,128)(2,1)S(1)}, bf16[1,1,4,64,128]{4,0,3,2,1:T(2,128)(2,1)S(1)}, u32[]{:S(2)}, u32[]{:S(2)}) collective-permute-start(bf16[1,1,4,64,128]{4,0,3,2,1:T(2,128)(2,1)S(1)} %copy.263), channel_id=1, source_target_pairs={{0,1},{1,2},{2,3},{3,4},{4,5},{5,6},{6,7},{7,8},{8,9},{9,10},{10,1... | collective-permute-start | bytes 196616 | tf_op jit(solution)/shard_map/ppermute | solution.py:30
  19.4 0.7 copy-start.1
  19.4 150.9 %copy-start.7 = (f32[256]{0:T(256)S(1)}, f32[256]{0:T(256)}, u32[]{:S(2)}) copy-start(f32[256]{0:T(256)} %param.12) | copy-start | bytes 3076
  19.4 150.9 %copy-start.9 = (f32[256]{0:T(256)S(1)}, f32[256]{0:T(256)}, u32[]{:S(2)}) copy-start(f32[256]{0:T(256)} %param.13) | copy-start | bytes 3076
  20.5 160.0 %copy-start.5 = (bf16[3,3,3,8,4]{3,4,2,1,0:T(4,128)(2,1)S(1)}, bf16[3,3,3,8,4]{3,4,2,1,0:T(4,128)(2,1)}, u32[]{:S(2)}) copy-start(bf16[3,3,3,8,4]{3,4,2,1,0:T(4,128)(2,1)} %param.14) | copy-start | bytes 5188
  20.5 160.0 %copy-start.12 = (u32[256]{0:T(256)S(1)}, u32[256]{0:T(256)}, u32[]{:S(2)}) copy-start(u32[256]{0:T(256)} %constant.108) | copy-start | bytes 3076
  172.4 16.9 %all-to-all-start = ((bf16[64,2,256]{2,1,0:T(2,128)(2,1)}), bf16[64,2,256]{2,1,0:T(2,128)(2,1)S(1)}, u32[]{:S(2)}, u32[]{:S(2)}) async-start(bf16[64,2,256]{2,1,0:T(2,128)(2,1)} %reshape.178), calls=%async_computation | async-start | bytes 131072 | tf_op jit(solution)/shard_map/all_to_all | solution.py:101
  198.3 25.6 %copy-start.8 = (f32[4]{0:T(128)S(1)}, f32[4]{0:T(128)}, u32[]{:S(2)}) copy-start(f32[4]{0:T(128)} %param.15) | copy-start | bytes 52
  198.3 25.6 %copy-start.10 = (f32[4]{0:T(128)S(1)}, f32[4]{0:T(128)}, u32[]{:S(2)}) copy-start(f32[4]{0:T(128)} %param.16) | copy-start | bytes 52
  198.3 26.4 %copy-start.4 = (bf16[1,4,64,2,32]{2,4,3,1,0:T(8,128)(2,1)S(1)}, bf16[1,4,64,2,32]{2,4,3,1,0:T(8,128)(2,1)}, u32[]{:S(2)}) copy-start(bf16[1,4,64,2,32]{2,4,3,1,0:T(8,128)(2,1)} %param.17) | copy-start | bytes 98308
  242.0 9.5 %copy-start.2 = (f32[1,2,8,5,256]{4,2,3,1,0:T(8,128)S(1)}, f32[1,2,8,5,256]{4,2,3,1,0:T(8,128)}, u32[]{:S(2)}) copy-start(f32[1,2,8,5,256]{4,2,3,1,0:T(8,128)} %get-tuple-element.280) | copy-start | bytes 245764
  245.9 14.9 %all-to-all-start.1 = ((f32[64,1,512]{2,1,0:T(1,128)}), f32[64,1,512]{2,1,0:T(1,128)S(1)}, u32[]{:S(2)}, u32[]{:S(2)}) async-start(f32[64,1,512]{2,1,0:T(1,128)} %reshape.180), calls=%async_computation.1 | async-start | bytes 262144 | tf_op jit(solution)/shard_map/all_to_all | solution.py:159
  251.4 458.0 %all-reduce.9.cloned.1.call-start = ((), (), s32[]{:S(2)}) async-start(), calls=%async_computation.2 | async-start | bytes 9437184
  340.2 78.3 %collective-permute-start.1 = (f32[3,3,3,128,256]{4,3,2,1,0:T(8,128)S(1)}, f32[3,3,3,128,256]{4,3,2,1,0:T(8,128)S(1)}, u32[]{:S(2)}, u32[]{:S(2)}) collective-permute-start(f32[3,3,3,128,256]{4,3,2,1,0:T(8,128)S(1)} %fusion.53), channel_id=1, source_target_pairs={{0,64},{64,0},{128,192},{192,128},{1,65},{65,1},{129,193},{193,129... | collective-permute-start | bytes 10616840 | tf_op jit(solution)/shard_map/ppermute | solution.py:19
  419.2 88.7 %collective-permute-start.2 = (f32[3,3,3,128,256]{4,3,2,1,0:T(8,128)S(1)}, f32[3,3,3,128,256]{4,3,2,1,0:T(8,128)S(1)}, u32[]{:S(2)}, u32[]{:S(2)}) collective-permute-start(f32[3,3,3,128,256]{4,3,2,1,0:T(8,128)S(1)} %add.153), channel_id=1, source_target_pairs={{0,128},{64,192},{128,0},{192,64},{1,129},{65,193},{129,1},{193,65... | collective-permute-start | bytes 10616840 | tf_op jit(solution)/shard_map/ppermute | solution.py:19
  516.4 0.7 copy-start.11
  516.5 5.3 copy-start.3
Sparse Core Ops, SparseCore 0:
  516.6 192.7 all-reduce.8
